TPU v7x, 128 devices: a whole 4x4x4 slice. The times are simulated.
128 devices in a mesh: depth: 4 (over x), panel: 32 (over y, z, core).
Axes of the slice: x: 4, y: 4, z: 4, core: 2. Of those that a mesh axis runs over, the one named last changes fastest.
Arguments:
- diag_blocks: float32 [4, 1024, 1024], P('depth', 'panel'), as said below
- coupling: float32 [4, 1024, 1024], P('depth', 'panel'), may hold values from -0.078125 to 0.078125
- sources: float32 [4, 1024, 256], P('depth', 'panel'), may hold values from -6 to 6
- requests: int32 [4, 128], P('depth', 'panel'), may hold values from 0 to 1023, as said below
Outputs:
- panels: float32 [4, 1024, 256], P('depth', 'panel')
- picked: float32 [4, 128, 256], P('depth', 'panel')
Inputs may be any that keep to these rules, and one draw needn't show every extreme that they name: `requests`: row numbers within their block; both 0 and 1023 occur. `diag_blocks`: every diagonal block is exactly symmetric with a positive diagonal.
All inputs are finite; a program needn't handle non-finite values.
Results may differ from a plain program's by a relative error of at most 0.0001.
Values sent between devices are 32-bit elements; how exact they have to be, the bound alone decides.
No kernel may reach another device: no remote copies, remote signals or barrier semaphores. Data moves between devices by JAX's collectives and lax.ppermute only.
A program may use at most 64 MiB of HBM per device.

v0:
```python
import jax
import jax.numpy as jnp
from jax import lax
from jax.sharding import PartitionSpec as P

ITERS = 2
highest = lax.Precision.HIGHEST


def passed_along(block, axis, distance):
    devices = range(lax.axis_size(axis))
    route = [(i - distance, i) for i in devices if i - distance in devices]
    return lax.ppermute(block, axis, route)


def product_rows(matrix, panel_rows):
    initial = jnp.zeros((matrix.shape[0], panel_rows.shape[1]), jnp.float32)
    shard_rows = lax.all_gather(panel_rows, "panel", axis=0, tiled=True)
    columns = lax.slice_in_dim(matrix, 0, shard_rows.shape[0], axis=1)
    return initial + jnp.dot(
        columns, shard_rows, precision=highest, preferred_element_type=jnp.float32
    )


def product_transposed(matrix, panel_rows):
    return lax.psum_scatter(
        lax.dot_general(
            matrix,
            panel_rows,
            (((0,), (0,)), ((), ())),
            precision=highest,
            preferred_element_type=jnp.float32,
        ),
        "panel",
        scatter_dimension=0,
        tiled=True,
    )


def jacobi(matrix, diag_part, right_hand):
    scaled = diag_part[:, None]
    iterate = right_hand / scaled
    for sweep_no in range(ITERS):
        image = product_rows(matrix, iterate)
        iterate = iterate + (right_hand - image) / scaled
    return iterate


def per_device(diag_blocks, coupling, sources, requests):
    depth_count = lax.axis_size("depth")
    depth_pos = lax.axis_index("depth")
    panel_pos = lax.axis_index("panel")
    block_count = diag_blocks.shape[0]
    row_count = diag_blocks.shape[1]
    local_cols = sources.shape[2]
    own_square = lax.dynamic_slice_in_dim(diag_blocks, panel_pos * row_count, row_count, 2)
    diag_part = jnp.diagonal(own_square, axis1=1, axis2=2)
    col_groups = 1
    col_width = local_cols // col_groups
    section_total = depth_count + col_groups - 1
    left_terms = jnp.zeros_like(sources)
    carried = jnp.zeros((row_count, col_width), jnp.float32)
    for section_no in range(section_total):
        column_pos = section_no - depth_pos
        active = (column_pos >= 0) & (column_pos < col_groups)
        col_start = jnp.clip(column_pos, 0, col_groups - 1) * col_width
        block_no = 0
        source_cols = sources[block_no]
        stored = lax.dynamic_update_slice_in_dim(left_terms[block_no], carried, col_start, 1)
        left_terms = left_terms.at[block_no].set(jnp.where(active, stored, left_terms[block_no]))
        forward = jacobi(diag_blocks[block_no], diag_part[block_no], source_cols - carried)
        carried = product_transposed(coupling[block_no], forward)
        carried = passed_along(carried, "depth", 1)
    panels = jnp.zeros_like(sources)
    ahead = jnp.zeros((row_count, col_width), jnp.float32)
    for section_no in range(section_total):
        column_pos = section_no - (depth_count - 1 - depth_pos)
        active = (column_pos >= 0) & (column_pos < col_groups)
        col_start = jnp.clip(column_pos, 0, col_groups - 1) * col_width
        for block_no in reversed(range(block_count)):
            source_cols = sources[block_no]
            left_cols = left_terms[block_no]
            right_term = product_rows(coupling[block_no], ahead)
            ahead = jacobi(
                diag_blocks[block_no], diag_part[block_no], source_cols - left_cols - right_term
            )
            stored = lax.dynamic_update_slice_in_dim(panels[block_no], ahead, col_start, 1)
            panels = panels.at[block_no].set(jnp.where(active, stored, panels[block_no]))
        ahead = passed_along(ahead, "depth", -1)
    picked_rows = requests.shape[1]
    shard_rows = lax.all_gather(panels, "panel", axis=1, tiled=True)
    shard_len = shard_rows.shape[1]
    inside = (requests >= 0) & (requests < shard_len)
    clipped = jnp.clip(requests, 0, shard_len - 1)
    where_rows = jnp.broadcast_to(
        clipped[:, :, None], (block_count, picked_rows, shard_rows.shape[2])
    )
    taken = jnp.take_along_axis(shard_rows, where_rows, axis=1)
    picked = jnp.where(inside[:, :, None], taken, 0.0)
    return (panels, picked)


def solution(mesh):
    placed = (
        P("depth", "panel", None),
        P("depth", "panel", None),
        P("depth", "panel", None),
        P("depth", "panel"),
    )
    return jax.shard_map(
        per_device,
        mesh=mesh,
        in_specs=placed,
        out_specs=(P("depth", "panel", None), P("depth", "panel", None)),
        check_vma=False,
    )
```

profile of v0, /device:TPU:1, one launch (start us, length us, event | category | flops | bytes accessed | tf_op | source)
XLA Modules:
  0.0 1144.0 jit_solution(601774973997432605)
XLA Ops:
  9.7 47.5 %all-gather.20.cloned.1.call-done = f32[1024,256]{1,0:T(8,128)} async-done(((f32[32,256]{1,0:T(8,128)}), f32[1024,256]{1,0:T(8,128)}) %all-gather.20.cloned.1.call-update) | async-done | bytes 1048592 | tf_op jit(solution)/shard_map/all_gather | solution.py:18
  57.1 2.5 fusion.45
  59.7 42.2 %all-gather.22.cloned.1.call-done = f32[1024,256]{1,0:T(8,128)} async-done(((f32[32,256]{1,0:T(8,128)}), f32[1024,256]{1,0:T(8,128)}) %all-gather.22.cloned.1.call-update) | async-done | bytes 1048592 | tf_op jit(solution)/shard_map/all_gather | solution.py:18
  102.0 1.9 fusion.42
  103.8 2.0 convolution_bitcast_fusion.2
  105.9 75.1 %reduce-scatter.4.cloned.1.call-done = f32[32,256]{1,0:T(8,128)} async-done(((f32[1024,256]{1,0:T(8,128)}), f32[32,256]{1,0:T(8,128)}) %reduce-scatter.4.cloned.1.call-update) | async-done | bytes 32784 | tf_op jit(solution)/shard_map/reduce_scatter | solution.py:26
  181.1 3.1 collective-permute-start
  186.2 45.9 %all-gather.24.cloned.1.call-done = f32[1024,256]{1,0:T(8,128)} async-done(((f32[32,256]{1,0:T(8,128)}), f32[1024,256]{1,0:T(8,128)}) %all-gather.24.cloned.1.call-update) | async-done | bytes 1048592 | tf_op jit(solution)/shard_map/all_gather | solution.py:18
  232.1 2.5 fusion.39
  234.7 42.1 %all-gather.26.cloned.1.call-done = f32[1024,256]{1,0:T(8,128)} async-done(((f32[32,256]{1,0:T(8,128)}), f32[1024,256]{1,0:T(8,128)}) %all-gather.26.cloned.1.call-update) | async-done | bytes 1048592 | tf_op jit(solution)/shard_map/all_gather | solution.py:18
  276.8 1.9 fusion.36
  278.7 2.0 convolution_bitcast_fusion.1
  280.8 75.1 %reduce-scatter.6.cloned.1.call-done = f32[32,256]{1,0:T(8,128)} async-done(((f32[1024,256]{1,0:T(8,128)}), f32[32,256]{1,0:T(8,128)}) %reduce-scatter.6.cloned.1.call-update) | async-done | bytes 32784 | tf_op jit(solution)/shard_map/reduce_scatter | solution.py:26
  355.9 3.1 collective-permute-start.1
  361.0 45.9 %all-gather.28.cloned.1.call-done = f32[1024,256]{1,0:T(8,128)} async-done(((f32[32,256]{1,0:T(8,128)}), f32[1024,256]{1,0:T(8,128)}) %all-gather.28.cloned.1.call-update) | async-done | bytes 1048592 | tf_op jit(solution)/shard_map/all_gather | solution.py:18
  406.9 2.5 fusion.33
  409.5 42.2 %all-gather.30.cloned.1.call-done = f32[1024,256]{1,0:T(8,128)} async-done(((f32[32,256]{1,0:T(8,128)}), f32[1024,256]{1,0:T(8,128)}) %all-gather.30.cloned.1.call-update) | async-done | bytes 1048592 | tf_op jit(solution)/shard_map/all_gather | solution.py:18
  451.8 1.9 fusion.30
  453.6 2.0 convolution_bitcast_fusion
  455.7 75.1 %reduce-scatter.8.cloned.1.call-done = f32[32,256]{1,0:T(8,128)} async-done(((f32[1024,256]{1,0:T(8,128)}), f32[32,256]{1,0:T(8,128)}) %reduce-scatter.8.cloned.1.call-update) | async-done | bytes 32784 | tf_op jit(solution)/shard_map/reduce_scatter | solution.py:26
  530.9 3.1 collective-permute-start.2
  536.0 45.9 %all-gather.32.cloned.1.call-done = f32[1024,256]{1,0:T(8,128)} async-done(((f32[32,256]{1,0:T(8,128)}), f32[1024,256]{1,0:T(8,128)}) %all-gather.32.cloned.1.call-update) | async-done | bytes 1048592 | tf_op jit(solution)/shard_map/all_gather | solution.py:18
  581.9 2.5 fusion.27
  584.5 42.3 %all-gather.34.cloned.1.call-done = f32[1024,256]{1,0:T(8,128)} async-done(((f32[32,256]{1,0:T(8,128)}), f32[1024,256]{1,0:T(8,128)}) %all-gather.34.cloned.1.call-update) | async-done | bytes 1048592 | tf_op jit(solution)/shard_map/all_gather | solution.py:18
  626.7 1.9 fusion.24
  629.9 3.4 collective-permute-done.3
  634.0 43.2 %all-gather.36.cloned.1.call-done = f32[1024,256]{1,0:T(8,128)} async-done(((f32[32,256]{1,0:T(8,128)}), f32[1024,256]{1,0:T(8,128)}) %all-gather.36.cloned.1.call-update) | async-done | bytes 1048592 | tf_op jit(solution)/shard_map/all_gather | solution.py:18
  677.2 2.5 broadcast_divide_fusion.2
  679.7 42.2 %all-gather.38.cloned.1.call-done = f32[1024,256]{1,0:T(8,128)} async-done(((f32[32,256]{1,0:T(8,128)}), f32[1024,256]{1,0:T(8,128)}) %all-gather.38.cloned.1.call-update) | async-done | bytes 1048592 | tf_op jit(solution)/shard_map/all_gather | solution.py:18
  722.0 2.5 fusion.20
  724.5 42.1 %all-gather.40.cloned.1.call-done = f32[1024,256]{1,0:T(8,128)} async-done(((f32[32,256]{1,0:T(8,128)}), f32[1024,256]{1,0:T(8,128)}) %all-gather.40.cloned.1.call-update) | async-done | bytes 1048592 | tf_op jit(solution)/shard_map/all_gather | solution.py:18
  766.7 1.9 fusion.17
  769.8 3.4 collective-permute-done.4
  773.9 43.2 %all-gather.42.cloned.1.call-done = f32[1024,256]{1,0:T(8,128)} async-done(((f32[32,256]{1,0:T(8,128)}), f32[1024,256]{1,0:T(8,128)}) %all-gather.42.cloned.1.call-update) | async-done | bytes 1048592 | tf_op jit(solution)/shard_map/all_gather | solution.py:18
  817.1 2.5 broadcast_divide_fusion.1
  819.8 41.9 %all-gather.44.cloned.1.call-done = f32[1024,256]{1,0:T(8,128)} async-done(((f32[32,256]{1,0:T(8,128)}), f32[1024,256]{1,0:T(8,128)}) %all-gather.44.cloned.1.call-update) | async-done | bytes 1048592 | tf_op jit(solution)/shard_map/all_gather | solution.py:18
  861.8 2.5 fusion.13
  864.3 42.1 %all-gather.46.cloned.1.call-done = f32[1024,256]{1,0:T(8,128)} async-done(((f32[32,256]{1,0:T(8,128)}), f32[1024,256]{1,0:T(8,128)}) %all-gather.46.cloned.1.call-update) | async-done | bytes 1048592 | tf_op jit(solution)/shard_map/all_gather | solution.py:18
  906.4 1.9 fusion.10
  909.6 3.4 collective-permute-done.5
  913.6 43.2 %all-gather.48.cloned.1.call-done = f32[1024,256]{1,0:T(8,128)} async-done(((f32[32,256]{1,0:T(8,128)}), f32[1024,256]{1,0:T(8,128)}) %all-gather.48.cloned.1.call-update) | async-done | bytes 1048592 | tf_op jit(solution)/shard_map/all_gather | solution.py:18
  956.8 2.5 broadcast_divide_fusion
  959.4 42.2 %all-gather.50.cloned.1.call-done = f32[1024,256]{1,0:T(8,128)} async-done(((f32[32,256]{1,0:T(8,128)}), f32[1024,256]{1,0:T(8,128)}) %all-gather.50.cloned.1.call-update) | async-done | bytes 1048592 | tf_op jit(solution)/shard_map/all_gather | solution.py:18
  1001.7 2.5 fusion.6
  1004.2 42.1 %all-gather.52.cloned.1.call-done = f32[1024,256]{1,0:T(8,128)} async-done(((f32[32,256]{1,0:T(8,128)}), f32[1024,256]{1,0:T(8,128)}) %all-gather.52.cloned.1.call-update) | async-done | bytes 1048592 | tf_op jit(solution)/shard_map/all_gather | solution.py:18
  1046.3 2.5 fusion.3
  1049.6 41.5 %all-gather.54.cloned.1.call-done = f32[1024,256]{1,0:T(8,128)} async-done(((f32[32,256]{1,0:T(8,128)}), f32[1024,256]{1,0:T(8,128)}) %all-gather.54.cloned.1.call-update) | async-done | bytes 1048592 | tf_op jit(solution)/shard_map/all_gather | solution.py:91
  1091.1 45.4 %gather_fusion.1 = f32[1024]{0:T(1024)S(1)} fusion(f32[1024,256]{1,0:T(8,128)} %all-gather.54.cloned.1.call-done, s32[1024]{0:T(1024)S(1)} %bitcast.246), kind=kCustom, calls=%fused_computation.1 | custom fusion | bytes 16384 | tf_op jit(solution)/shard_map/jit(take_along_axis)/gather | solution.py:98
  (92 shorter events, 16.9 us)
Async XLA Ops:
  7.2 0.9 copy-start
  7.2 50.0 %all-gather.20.cloned.1.call-start = ((), (), s32[]{:S(2)}) async-start(), calls=%async_computation.3 | async-start | bytes 1081344 | tf_op jit(solution)/shard_map/all_gather | solution.py:18
  8.1 0.8 copy-start.2
  9.6 92.3 %all-gather.22.cloned.1.call-start = ((), (), s32[]{:S(2)}) async-start(), calls=%async_computation.4 | async-start | bytes 1081344 | tf_op jit(solution)/shard_map/all_gather | solution.py:18
  59.6 42.3 %copy-start.7 = (f32[32,256]{1,0:T(8,128)S(1)}, f32[32,256]{1,0:T(8,128)}, u32[]{:S(2)}) copy-start(f32[32,256]{1,0:T(8,128)} %fusion.45) | copy-start | bytes 98308
  59.7 44.2 %copy-start.1 = (f32[1,32,1024]{2,1,0:T(8,128)S(1)}, f32[1,32,1024]{2,1,0:T(8,128)}, u32[]{:S(2)}) copy-start(f32[1,32,1024]{2,1,0:T(8,128)} %param.21) | copy-start | bytes 393220
  59.7 121.4 %reduce-scatter.4.cloned.1.call-start = ((), (), s32[]{:S(2)}) async-start(), calls=%async_computation.5 | async-start | bytes 1081344 | tf_op jit(solution)/shard_map/reduce_scatter | solution.py:26
  105.9 126.2 %all-gather.24.cloned.1.call-start = ((), (), s32[]{:S(2)}) async-start(), calls=%async_computation.6 | async-start | bytes 1081344 | tf_op jit(solution)/shard_map/all_gather | solution.py:18
  181.1 4.4 collective-permute-start
  186.2 90.6 %all-gather.26.cloned.1.call-start = ((), (), s32[]{:S(2)}) async-start(), calls=%async_computation.7 | async-start | bytes 1081344 | tf_op jit(solution)/shard_map/all_gather | solution.py:18
  234.6 42.2 %copy-start.8 = (f32[32,256]{1,0:T(8,128)S(1)}, f32[32,256]{1,0:T(8,128)}, u32[]{:S(2)}) copy-start(f32[32,256]{1,0:T(8,128)} %fusion.39) | copy-start | bytes 98308
  234.6 121.2 %reduce-scatter.6.cloned.1.call-start = ((), (), s32[]{:S(2)}) async-start(), calls=%async_computation.8 | async-start | bytes 1081344 | tf_op jit(solution)/shard_map/reduce_scatter | solution.py:26
  280.7 126.2 %all-gather.28.cloned.1.call-start = ((), (), s32[]{:S(2)}) async-start(), calls=%async_computation.9 | async-start | bytes 1081344 | tf_op jit(solution)/shard_map/all_gather | solution.py:18
  355.9 4.4 collective-permute-start.1
  361.0 90.8 %all-gather.30.cloned.1.call-start = ((), (), s32[]{:S(2)}) async-start(), calls=%async_computation.10 | async-start | bytes 1081344 | tf_op jit(solution)/shard_map/all_gather | solution.py:18
  409.4 42.3 %copy-start.9 = (f32[32,256]{1,0:T(8,128)S(1)}, f32[32,256]{1,0:T(8,128)}, u32[]{:S(2)}) copy-start(f32[32,256]{1,0:T(8,128)} %fusion.33) | copy-start | bytes 98308
  409.5 121.4 %reduce-scatter.8.cloned.1.call-start = ((), (), s32[]{:S(2)}) async-start(), calls=%async_computation.11 | async-start | bytes 1081344 | tf_op jit(solution)/shard_map/reduce_scatter | solution.py:26
  455.7 126.2 %all-gather.32.cloned.1.call-start = ((), (), s32[]{:S(2)}) async-start(), calls=%async_computation.12 | async-start | bytes 1081344 | tf_op jit(solution)/shard_map/all_gather | solution.py:18
  530.9 4.4 collective-permute-start.2
  536.0 90.8 %all-gather.34.cloned.1.call-start = ((), (), s32[]{:S(2)}) async-start(), calls=%async_computation.13 | async-start | bytes 1081344 | tf_op jit(solution)/shard_map/all_gather | solution.py:18
  584.4 42.3 %copy-start.4 = (f32[32,256]{1,0:T(8,128)S(1)}, f32[32,256]{1,0:T(8,128)}, u32[]{:S(2)}) copy-start(f32[32,256]{1,0:T(8,128)} %fusion.27) | copy-start | bytes 98308
  584.4 92.7 %all-gather.36.cloned.1.call-start = ((), (), s32[]{:S(2)}) async-start(), calls=%async_computation.14 | async-start | bytes 1081344 | tf_op jit(solution)/shard_map/all_gather | solution.py:18
  628.6 4.7 collective-permute-start.3
  633.3 0.6 copy-start.10
  633.9 88.1 %all-gather.38.cloned.1.call-start = ((), (), s32[]{:S(2)}) async-start(), calls=%async_computation.15 | async-start | bytes 1081344 | tf_op jit(solution)/shard_map/all_gather | solution.py:18
  679.7 87.0 %all-gather.40.cloned.1.call-start = ((), (), s32[]{:S(2)}) async-start(), calls=%async_computation.16 | async-start | bytes 1081344 | tf_op jit(solution)/shard_map/all_gather | solution.py:18
  724.5 42.2 %copy-start.5 = (f32[32,256]{1,0:T(8,128)S(1)}, f32[32,256]{1,0:T(8,128)}, u32[]{:S(2)}) copy-start(f32[32,256]{1,0:T(8,128)} %fusion.20) | copy-start | bytes 98308
  724.5 92.6 %all-gather.42.cloned.1.call-start = ((), (), s32[]{:S(2)}) async-start(), calls=%async_computation.17 | async-start | bytes 1081344 | tf_op jit(solution)/shard_map/all_gather | solution.py:18
  768.5 4.7 collective-permute-start.4
  773.2 0.6 copy-start.11
  773.8 87.9 %all-gather.44.cloned.1.call-start = ((), (), s32[]{:S(2)}) async-start(), calls=%async_computation.18 | async-start | bytes 1081344 | tf_op jit(solution)/shard_map/all_gather | solution.py:18
  819.6 86.8 %all-gather.46.cloned.1.call-start = ((), (), s32[]{:S(2)}) async-start(), calls=%async_computation.19 | async-start | bytes 1081344 | tf_op jit(solution)/shard_map/all_gather | solution.py:18
  864.2 42.2 %copy-start.6 = (f32[32,256]{1,0:T(8,128)S(1)}, f32[32,256]{1,0:T(8,128)}, u32[]{:S(2)}) copy-start(f32[32,256]{1,0:T(8,128)} %fusion.13) | copy-start | bytes 98308
  864.3 92.6 %all-gather.48.cloned.1.call-start = ((), (), s32[]{:S(2)}) async-start(), calls=%async_computation.20 | async-start | bytes 1081344 | tf_op jit(solution)/shard_map/all_gather | solution.py:18
  908.3 4.7 collective-permute-start.5
  913.0 0.6 copy-start.12
  913.6 88.1 %all-gather.50.cloned.1.call-start = ((), (), s32[]{:S(2)}) async-start(), calls=%async_computation.21 | async-start | bytes 1081344 | tf_op jit(solution)/shard_map/all_gather | solution.py:18
  959.4 87.0 %all-gather.52.cloned.1.call-start = ((), (), s32[]{:S(2)}) async-start(), calls=%async_computation.22 | async-start | bytes 1081344 | tf_op jit(solution)/shard_map/all_gather | solution.py:18
  1004.1 42.2 %copy-start.3 = (f32[32,256]{1,0:T(8,128)S(1)}, f32[32,256]{1,0:T(8,128)}, u32[]{:S(2)}) copy-start(f32[32,256]{1,0:T(8,128)} %fusion.6) | copy-start | bytes 98308
  1004.2 87.0 %all-gather.54.cloned.1.call-start = ((), (), s32[]{:S(2)}) async-start(), calls=%async_computation.23 | async-start | bytes 1081344 | tf_op jit(solution)/shard_map/all_gather | solution.py:91
  1048.8 0.7 copy-start.13
Sparse Core Ops, SparseCore 0:
  10.8 46.2 all-gather.19
  60.0 41.9 all-gather.21
  106.0 74.9 reduce-scatter.3
  186.3 45.7 all-gather.23
  234.8 41.9 all-gather.25
  280.8 74.9 reduce-scatter.5
  361.1 45.7 all-gather.27
  409.8 41.9 all-gather.29
  455.8 74.9 reduce-scatter.7
  536.1 45.7 all-gather.31
  584.8 41.9 all-gather.33
  634.0 43.0 all-gather.35
  680.0 41.9 all-gather.37
  724.7 41.9 all-gather.39
  774.0 43.0 all-gather.41
  819.8 41.9 all-gather.43
  864.4 41.9 all-gather.45
  913.7 43.0 all-gather.47
  959.7 41.9 all-gather.49
  1004.3 41.9 all-gather.51
  1049.2 41.9 all-gather.53
where the time goes:
time: 1150 us; the launch traced here: 1140 us
  waiting for transfers between devices  1020 us (89%)
  local copies, waits for them, and re-layouts  49.6 us (4%)
  matrix products  44.8 us (4%)
  between operations  14.6 us (1%)
  starting transfers between devices  14.2 us (1%)
    all_gather x17, waiting for transfers between devices, product_rows(): shard_rows = lax.all_gather(panel_rows, 'panel', axis=0, tiled=True)  736 us
    reduce_scatter x3, waiting for transfers between devices, product_transposed(): lax.psum_scatter(lax.dot_general(matrix, panel_rows, (((0,), (0,)), ((),...  225 us
    gather x2, local copies, waits for them, and re-layouts, per_device(): taken = jnp.take_along_axis(shard_rows, where_rows, axis=1)  45.4 us
    all_gather x1, waiting for transfers between devices, per_device(): shard_rows = lax.all_gather(panels, 'panel', axis=1, tiled=True)  41.5 us
    dot_general x17, matrix products, product_rows(): jnp.dot(columns, shard_rows, precision=highest, preferred_element_type=jn...  38.7 us
  transfers between devices with their start and end apart: 27, of which 27 were waited for; matrix products, arithmetic and copies ran while one was open for 0% of the time, Pallas kernels for 0%

commit v1 on v0

--- a/solution.py
+++ b/solution.py
@@ -15,7 +15,9 @@
 
 def product_rows(matrix, panel_rows):
     initial = jnp.zeros((matrix.shape[0], panel_rows.shape[1]), jnp.float32)
-    shard_rows = lax.all_gather(panel_rows, "panel", axis=0, tiled=True)
+    shard_rows = jnp.concatenate(
+        lax.all_to_all(jnp.stack([panel_rows] * lax.axis_size("panel")), "panel", 0, 0), axis=0
+    )
     columns = lax.slice_in_dim(matrix, 0, shard_rows.shape[0], axis=1)
     return initial + jnp.dot(
         columns, shard_rows, precision=highest, preferred_element_type=jnp.float32

time: 1150 us -> 753 us (0.65)
  waiting for transfers between devices: 1020 us -> 296 us
  blocking collectives: 0 us -> 351 us
  matrix products: 44.8 us -> 17.7 us
    all_gather x17 -> x0, waiting for transfers between devices: 736 us -> none  [product_rows(): shard_rows = lax.all_gather(panel_rows, 'panel', axis=0, tiled=True)]
    all_to_all x0 -> x16, blocking collectives: none -> 351 us  [product_rows(): lax.all_to_all(jnp.stack([panel_rows] * lax.axis_size('panel')), 'panel',...]
    dot_general x17, matrix products: 38.7 us -> 11.7 us  [product_rows(): jnp.dot(columns, shard_rows, precision=highest, preferred_element_type=jn...]
    all_to_all x0 -> x1, waiting for transfers between devices: none -> 16.8 us  [product_rows(): lax.all_to_all(jnp.stack([panel_rows] * lax.axis_size('panel')), 'panel',...]
  transfers between devices with their start and end apart: 27 -> 11, of which waited for: 27 -> 11; matrix products, arithmetic and copies ran while one was open for 0% -> 0% of each run, Pallas kernels for 0% -> 0%
where the time goes in v1:
time: 753 us; the launch traced here: 748 us
  blocking collectives  351 us (47%)
  waiting for transfers between devices  296 us (39%)
  local copies, waits for them, and re-layouts  50.8 us (7%)
  matrix products  17.7 us (2%)
  starting transfers between devices  17.3 us (2%)
  between operations  14.2 us (2%)
    all_to_all x16, blocking collectives, product_rows(): lax.all_to_all(jnp.stack([panel_rows] * lax.axis_size('panel')), 'panel',...  351 us
    reduce_scatter x3, waiting for transfers between devices, product_transposed(): lax.psum_scatter(lax.dot_general(matrix, panel_rows, (((0,), (0,)), ((),...  223 us
    gather x2, local copies, waits for them, and re-layouts, per_device(): taken = jnp.take_along_axis(shard_rows, where_rows, axis=1)  45.4 us
    all_gather x1, waiting for transfers between devices, per_device(): shard_rows = lax.all_gather(panels, 'panel', axis=1, tiled=True)  40.5 us
    all_to_all x1, waiting for transfers between devices, product_rows(): lax.all_to_all(jnp.stack([panel_rows] * lax.axis_size('panel')), 'panel',...  16.8 us
    ppermute x6, waiting for transfers between devices, passed_along(): return lax.ppermute(block, axis, route)  16 us
  transfers between devices with their start and end apart: 11, of which 11 were waited for; matrix products, arithmetic and copies ran while one was open for 0% of the time, Pallas kernels for 0%

profile of v1, /device:TPU:1, one launch (start us, length us, event | category | flops | bytes accessed | tf_op | source)
XLA Modules:
  0.0 747.9 jit_solution(16065723720103580310)
XLA Ops:
  7.2 0.8 copy-done
  8.2 0.7 gather_fusion
  9.1 26.3 %all_to_all.86 = f32[32,32,256]{2,1,0:T(8,128)S(1)} all-to-all(f32[32,32,256]{2,1,0:T(8,128)S(1)} %stack.37), channel_id=1, replica_groups=mesh['depth'=4,'panel'=32] {'panel'}, dimensions={0} | all-to-all | bytes 2097152 | tf_op jit(solution)/shard_map/all_to_all | solution.py:19
  35.4 0.7 fusion.45
  36.2 20.6 %all_to_all.87 = f32[32,32,256]{2,1,0:T(8,128)S(1)} all-to-all(f32[32,32,256]{2,1,0:T(8,128)S(1)} %stack.38), channel_id=1, replica_groups=mesh['depth'=4,'panel'=32] {'panel'}, dimensions={0} | all-to-all | bytes 2097152 | tf_op jit(solution)/shard_map/all_to_all | solution.py:19
  57.7 2.0 convolution_bitcast_fusion.2
  59.8 73.7 %reduce-scatter.4.cloned.1.call-done = f32[32,256]{1,0:T(8,128)} async-done(((f32[1024,256]{1,0:T(8,128)}), f32[32,256]{1,0:T(8,128)}) %reduce-scatter.4.cloned.1.call-update) | async-done | bytes 32784 | tf_op jit(solution)/shard_map/reduce_scatter | solution.py:28
  133.5 3.1 collective-permute-start
  136.6 1.3 collective-permute-done
  138.1 25.1 %all_to_all.88 = f32[32,32,256]{2,1,0:T(8,128)S(1)} all-to-all(f32[32,32,256]{2,1,0:T(8,128)S(1)} %stack.39), channel_id=1, replica_groups=mesh['depth'=4,'panel'=32] {'panel'}, dimensions={0} | all-to-all | bytes 2097152 | tf_op jit(solution)/shard_map/all_to_all | solution.py:19
  164.0 20.6 %all_to_all.89 = f32[32,32,256]{2,1,0:T(8,128)S(1)} all-to-all(f32[32,32,256]{2,1,0:T(8,128)S(1)} %stack.40), channel_id=1, replica_groups=mesh['depth'=4,'panel'=32] {'panel'}, dimensions={0} | all-to-all | bytes 2097152 | tf_op jit(solution)/shard_map/all_to_all | solution.py:19
  185.3 2.0 convolution_bitcast_fusion.1
  187.4 74.4 %reduce-scatter.6.cloned.1.call-done = f32[32,256]{1,0:T(8,128)} async-done(((f32[1024,256]{1,0:T(8,128)}), f32[32,256]{1,0:T(8,128)}) %reduce-scatter.6.cloned.1.call-update) | async-done | bytes 32784 | tf_op jit(solution)/shard_map/reduce_scatter | solution.py:28
  261.8 3.1 collective-permute-start.1
  264.9 1.3 collective-permute-done.1
  266.4 25.1 %all_to_all.90 = f32[32,32,256]{2,1,0:T(8,128)S(1)} all-to-all(f32[32,32,256]{2,1,0:T(8,128)S(1)} %stack.41), channel_id=1, replica_groups=mesh['depth'=4,'panel'=32] {'panel'}, dimensions={0} | all-to-all | bytes 2097152 | tf_op jit(solution)/shard_map/all_to_all | solution.py:19
  292.3 20.6 %all_to_all.91 = f32[32,32,256]{2,1,0:T(8,128)S(1)} all-to-all(f32[32,32,256]{2,1,0:T(8,128)S(1)} %stack.42), channel_id=1, replica_groups=mesh['depth'=4,'panel'=32] {'panel'}, dimensions={0} | all-to-all | bytes 2097152 | tf_op jit(solution)/shard_map/all_to_all | solution.py:19
  312.9 0.7 fusion.30
  313.6 2.0 convolution_bitcast_fusion
  315.6 74.5 %reduce-scatter.8.cloned.1.call-done = f32[32,256]{1,0:T(8,128)} async-done(((f32[1024,256]{1,0:T(8,128)}), f32[32,256]{1,0:T(8,128)}) %reduce-scatter.8.cloned.1.call-update) | async-done | bytes 32784 | tf_op jit(solution)/shard_map/reduce_scatter | solution.py:28
  390.1 3.3 collective-permute-start.2
  393.5 1.2 collective-permute-done.2
  394.9 24.9 %all_to_all.92 = f32[32,32,256]{2,1,0:T(8,128)S(1)} all-to-all(f32[32,32,256]{2,1,0:T(8,128)S(1)} %stack.43), channel_id=1, replica_groups=mesh['depth'=4,'panel'=32] {'panel'}, dimensions={0} | all-to-all | bytes 2097152 | tf_op jit(solution)/shard_map/all_to_all | solution.py:19
  419.8 0.7 fusion.27
  420.6 20.6 %all_to_all.93 = f32[32,32,256]{2,1,0:T(8,128)S(1)} all-to-all(f32[32,32,256]{2,1,0:T(8,128)S(1)} %stack.44), channel_id=1, replica_groups=mesh['depth'=4,'panel'=32] {'panel'}, dimensions={0} | all-to-all | bytes 2097152 | tf_op jit(solution)/shard_map/all_to_all | solution.py:19
  441.9 1.3 collective-permute-start.3
  443.2 4.2 collective-permute-done.3
  447.5 21.2 %all_to_all.94 = f32[32,32,256]{2,1,0:T(8,128)S(1)} all-to-all(f32[32,32,256]{2,1,0:T(8,128)S(1)} %stack.45), channel_id=1, replica_groups=mesh['depth'=4,'panel'=32] {'panel'}, dimensions={0} | all-to-all | bytes 2097152 | tf_op jit(solution)/shard_map/all_to_all | solution.py:19
  469.4 20.6 %all_to_all.95 = f32[32,32,256]{2,1,0:T(8,128)S(1)} all-to-all(f32[32,32,256]{2,1,0:T(8,128)S(1)} %stack.46), channel_id=1, replica_groups=mesh['depth'=4,'panel'=32] {'panel'}, dimensions={0} | all-to-all | bytes 2097152 | tf_op jit(solution)/shard_map/all_to_all | solution.py:19
  490.9 20.6 %all_to_all.96 = f32[32,32,256]{2,1,0:T(8,128)S(1)} all-to-all(f32[32,32,256]{2,1,0:T(8,128)S(1)} %stack.47), channel_id=1, replica_groups=mesh['depth'=4,'panel'=32] {'panel'}, dimensions={0} | all-to-all | bytes 2097152 | tf_op jit(solution)/shard_map/all_to_all | solution.py:19
  512.2 1.3 collective-permute-start.4
  513.5 4.0 collective-permute-done.4
  517.6 21.2 %all_to_all.97 = f32[32,32,256]{2,1,0:T(8,128)S(1)} all-to-all(f32[32,32,256]{2,1,0:T(8,128)S(1)} %stack.48), channel_id=1, replica_groups=mesh['depth'=4,'panel'=32] {'panel'}, dimensions={0} | all-to-all | bytes 2097152 | tf_op jit(solution)/shard_map/all_to_all | solution.py:19
  539.5 20.6 %all_to_all.98 = f32[32,32,256]{2,1,0:T(8,128)S(1)} all-to-all(f32[32,32,256]{2,1,0:T(8,128)S(1)} %stack.49), channel_id=1, replica_groups=mesh['depth'=4,'panel'=32] {'panel'}, dimensions={0} | all-to-all | bytes 2097152 | tf_op jit(solution)/shard_map/all_to_all | solution.py:19
  560.9 20.6 %all_to_all.99 = f32[32,32,256]{2,1,0:T(8,128)S(1)} all-to-all(f32[32,32,256]{2,1,0:T(8,128)S(1)} %stack.50), channel_id=1, replica_groups=mesh['depth'=4,'panel'=32] {'panel'}, dimensions={0} | all-to-all | bytes 2097152 | tf_op jit(solution)/shard_map/all_to_all | solution.py:19
  581.5 0.7 fusion.10
  582.2 1.3 collective-permute-start.5
  583.5 4.0 collective-permute-done.5
  587.6 21.2 %all_to_all.100 = f32[32,32,256]{2,1,0:T(8,128)S(1)} all-to-all(f32[32,32,256]{2,1,0:T(8,128)S(1)} %stack.51), channel_id=1, replica_groups=mesh['depth'=4,'panel'=32] {'panel'}, dimensions={0} | all-to-all | bytes 2097152 | tf_op jit(solution)/shard_map/all_to_all | solution.py:19
  609.5 20.6 %all_to_all.101 = f32[32,32,256]{2,1,0:T(8,128)S(1)} all-to-all(f32[32,32,256]{2,1,0:T(8,128)S(1)} %stack.52), channel_id=1, replica_groups=mesh['depth'=4,'panel'=32] {'panel'}, dimensions={0} | all-to-all | bytes 2097152 | tf_op jit(solution)/shard_map/all_to_all | solution.py:19
  630.2 0.7 fusion.6
  630.8 1.1 stack.53
  631.9 3.9 all-to-all-start.16
  635.9 16.8 %all-to-all-done.16 = f32[32,32,256]{2,1,0:T(8,128)S(1)} async-done(((f32[32,32,256]{2,1,0:T(8,128)}), f32[32,32,256]{2,1,0:T(8,128)S(1)}, u32[]{:S(2)}, u32[]{:S(2)}) %all-to-all-start.16) | async-done | bytes 1048608 | tf_op jit(solution)/shard_map/all_to_all | solution.py:19
  652.8 1.3 fusion.3
  654.8 40.5 %all-gather.3.cloned.1.call-done = f32[1024,256]{1,0:T(8,128)} async-done(((f32[32,256]{1,0:T(8,128)}), f32[1024,256]{1,0:T(8,128)}) %all-gather.3.cloned.1.call-update) | async-done | bytes 1048592 | tf_op jit(solution)/shard_map/all_gather | solution.py:93
  695.3 45.4 %gather_fusion.1 = f32[1024]{0:T(1024)S(1)} fusion(f32[1024,256]{1,0:T(8,128)} %all-gather.3.cloned.1.call-done, s32[1024]{0:T(1024)S(1)} %bitcast.265), kind=kCustom, calls=%fused_computation.1 | custom fusion | bytes 16384 | tf_op jit(solution)/shard_map/jit(take_along_axis)/gather | solution.py:100
  740.7 0.7 select_select_fusion
  (56 shorter events, 10.7 us)
Async XLA Ops:
  7.2 0.9 copy-start
  7.2 126.4 %reduce-scatter.4.cloned.1.call-start = ((), (), s32[]{:S(2)}) async-start(), calls=%async_computation.20 | async-start | bytes 1081344 | tf_op jit(solution)/shard_map/reduce_scatter | solution.py:28
  8.1 0.8 copy-start.2
  56.8 0.9 copy-start.1
  59.7 202.1 %reduce-scatter.6.cloned.1.call-start = ((), (), s32[]{:S(2)}) async-start(), calls=%async_computation.21 | async-start | bytes 1081344 | tf_op jit(solution)/shard_map/reduce_scatter | solution.py:28
  133.5 4.4 collective-permute-start
  187.4 202.8 %reduce-scatter.8.cloned.1.call-start = ((), (), s32[]{:S(2)}) async-start(), calls=%async_computation.22 | async-start | bytes 1081344 | tf_op jit(solution)/shard_map/reduce_scatter | solution.py:28
  261.8 4.4 collective-permute-start.1
  390.1 4.6 collective-permute-start.2
  441.9 5.5 collective-permute-start.3
  512.2 5.3 collective-permute-start.4
  582.2 5.3 collective-permute-start.5
  631.9 20.8 %all-to-all-start.16 = ((f32[32,32,256]{2,1,0:T(8,128)}), f32[32,32,256]{2,1,0:T(8,128)S(1)}, u32[]{:S(2)}, u32[]{:S(2)}) async-start(f32[32,32,256]{2,1,0:T(8,128)} %stack.53), calls=%async_computation.19 | async-start | bytes 2097152 | tf_op jit(solution)/shard_map/all_to_all | solution.py:19
  635.9 59.5 %all-gather.3.cloned.1.call-start = ((), (), s32[]{:S(2)}) async-start(), calls=%async_computation.23 | async-start | bytes 1081344 | tf_op jit(solution)/shard_map/all_gather | solution.py:93
  654.0 0.7 copy-start.3
Sparse Core Ops, SparseCore 0:
  59.9 73.6 reduce-scatter.3
  187.5 74.2 reduce-scatter.5
  315.7 74.3 reduce-scatter.7
  654.2 41.1 all-gather.2
